TPU v7x, 32 devices: a whole 2x2x4 slice. The times are simulated.
32 devices in a mesh: pole: 4 (over x, core), row: 4 (over z), col: 2 (over y).
Axes of the slice: x: 2, y: 2, z: 4, core: 2. Of those that a mesh axis runs over, the one named last changes fastest.
Arguments:
- green: bfloat16 [4, 4096, 4096], P('pole', 'row', 'col'), may hold values from -6 to 6
- factor: bfloat16 [4, 4096, 1024], P('pole', 'row', 'col'), may hold values from -0.09375 to 0.09375
- diag_inverse: bfloat16 [4, 512, 1024], P('pole', 'row', 'col'), may hold values from -6 to 6
- pole_weight: float32 [4], P('pole'), may hold values from 0.25 to 1
- pattern: int32 [8, 2], replicated, may hold values 0 or 1
Outputs:
- off_density: float32 [4096, 1024], P(('row', 'pole'), 'col')
- diag_density: float32 [512, 1024], P(('pole', 'row'), 'col')
All inputs are finite; a program needn't handle non-finite values.
Results may differ from a plain program's by a relative error of at most 0.005.
Values may be sent and summed in bfloat16 or wider, within the bound.
No kernel may reach another device: no remote copies, remote signals or barrier semaphores. Data moves between devices by JAX's collectives and lax.ppermute only.
A program may use at most 64 MiB of HBM per device.

v0:
```python
import jax
import jax.numpy as jnp
from jax import lax
from jax.sharding import PartitionSpec as P

BLOCK = 512
ANC = 8


def body(green, factor, diag_inverse, pole_weight, pattern):
    poles_here = green.shape[0]
    local_rows = factor.shape[1]
    local_cols = factor.shape[2]
    level_count = pattern.shape[1]
    row_at = lax.axis_index("row")
    col_at = lax.axis_index("col")
    row_ids = (row_at * local_rows + jnp.arange(local_rows, dtype=jnp.int32)) // BLOCK
    col_ids = (col_at * local_cols + jnp.arange(local_cols, dtype=jnp.int32)) // BLOCK
    row_onehot = (row_ids[:, None] == jnp.arange(ANC, dtype=jnp.int32)[None, :]).astype(jnp.float32)
    col_onehot = (col_ids[:, None] == jnp.arange(level_count, dtype=jnp.int32)[None, :]).astype(
        jnp.float32
    )
    pattern_f = pattern.astype(jnp.float32)
    keep_mask = jnp.dot(jnp.dot(row_onehot, pattern_f), col_onehot.T)
    masked = factor * keep_mask.astype(jnp.bfloat16)[None]
    whole_rows = lax.all_gather(green, "col", axis=2, tiled=True)
    product = jnp.einsum(
        "pij,pjk->pik",
        whole_rows,
        lax.all_gather(masked, "row", axis=1, tiled=True),
        preferred_element_type=jnp.float32,
    )
    update = (product * keep_mask[None]).astype(jnp.bfloat16)
    weights = pole_weight[:, None, None]
    off_term = -jnp.sum(weights * update.astype(jnp.float32), axis=0)
    level_here = local_cols // BLOCK
    factor_split = masked.reshape(poles_here, local_rows, level_here, BLOCK)
    update_split = update.reshape(poles_here, local_rows, level_here, BLOCK)
    cross_term = jnp.einsum(
        "prka,prkb->pakb", factor_split, update_split, preferred_element_type=jnp.float32
    )
    cross_term = cross_term.reshape(poles_here, BLOCK, local_cols)
    diag_term = -jnp.sum(weights * cross_term, axis=0)
    dinv_count = diag_inverse.shape[1]
    dinv_rows = jnp.sum(weights * diag_inverse.astype(jnp.float32), axis=0)
    current = lax.dynamic_slice_in_dim(diag_term, row_at * dinv_count, dinv_count, 0)
    diag_term = lax.dynamic_update_slice_in_dim(
        diag_term, current + dinv_rows, row_at * dinv_count, 0
    )
    off_density, pole_part = (
        lax.psum_scatter(off_term, "pole", scatter_dimension=0, tiled=True),
        lax.psum_scatter(diag_term, "pole", scatter_dimension=0, tiled=True),
    )
    diag_density = lax.psum_scatter(pole_part, "row", scatter_dimension=0, tiled=True)
    return (off_density, diag_density)


def solution(mesh):
    in_specs = (
        P("pole", "row", "col"),
        P("pole", "row", "col"),
        P("pole", "row", "col"),
        P("pole"),
        P(),
    )
    out_specs = (P(("row", "pole"), "col"), P(("pole", "row"), "col"))
    return jax.shard_map(body, mesh=mesh, in_specs=in_specs, out_specs=out_specs, check_vma=False)
```

profile of v0, /device:TPU:0, one launch (start us, length us, event | category | flops | bytes accessed | tf_op | source)
XLA Modules:
  0.0 296.8 jit_solution(12370110417123104437)
XLA Ops:
  7.2 0.0 all-gather.3.cloned.1.call-start
  7.3 2.9 bitcast_multiply_fusion.1
  10.1 0.0 all-gather.3.cloned.1.call-update
  10.2 0.0 copy-start.2
  10.2 0.0 all-gather.5.cloned.1.call-start
  10.2 0.7 all-gather.5.cloned.1.call-update
  10.9 0.0 reduce-scatter.8.cloned.1.call-start
  11.6 0.0 copy-done.2
  11.6 0.1 copy.11
  11.8 82.0 %all-gather.3.cloned.1.call-done = bf16[1,4096,512]{2,1,0:T(8,128)(2,1)} async-done(((bf16[1,1024,512]{2,1,0:T(8,128)(2,1)}), bf16[1,4096,512]{2,1,0:T(8,128)(2,1)}) %all-gather.3.cloned.1.call-update) | async-done | bytes 4194320 | tf_op jit(solution)/shard_map/all_gather | solution.py:30
  93.8 104.0 %all-gather.5.cloned.1.call-done = bf16[1,1024,4096]{2,1,0:T(8,128)(2,1)} async-done(((bf16[1,1024,2048]{2,1,0:T(8,128)(2,1)}), bf16[1,1024,4096]{2,1,0:T(8,128)(2,1)}) %all-gather.5.cloned.1.call-update) | async-done | bytes 8388624 | tf_op jit(solution)/shard_map/all_gather | solution.py:26
  197.8 0.0 copy-start
  197.8 10.5 %multiply_negate_fusion = (f32[1024,512]{1,0:T(8,128)}, bf16[1024,512]{1,0:T(8,128)(2,1)S(1)}) fusion(f32[]{:T(128)} %bitcast.41, f32[1024,512]{1,0:T(8,128)S(1)} %get-tuple-element.7, bf16[1,4096,512]{2,1,0:T(8,128)(2,1)} %all-gather.3.cloned.1.call-done, bf16[1,1024,4096]{2,1,0:T(8,128)(2,1)} %all-gather.5.cloned.1.call-done), kind=kOutput, calls=%fused_computation.5 | convolution fusion | flops 4297588736 | bytes 17825796 | tf_op jit(solution)/shard_map/pij,pjk->pik/dot_general | solution.py:27
  208.3 0.0 copy-done
  208.3 0.7 fusion.8
  209.0 0.1 copy.16
  209.2 0.0 copy-start.1
  209.2 1.0 copy-done.1
  210.2 0.0 reduce-scatter.8.cloned.1.call-update
  210.2 0.0 reduce-scatter.10.cloned.1.call-start
  210.2 24.9 %reduce-scatter.8.cloned.1.call-done = f32[128,512]{0,1:T(8,128)} async-done(((f32[512,512]{0,1:T(8,128)}), f32[128,512]{0,1:T(8,128)}) %reduce-scatter.8.cloned.1.call-update) | async-done | bytes 262160 | tf_op jit(solution)/shard_map/reduce_scatter | solution.py:52
  235.2 1.8 copy.14
  236.9 0.0 reduce-scatter.10.cloned.1.call-update
  237.0 0.0 reduce-scatter.6.cloned.1.call-start
  237.0 0.5 reduce-scatter.6.cloned.1.call-update
  237.6 20.3 %reduce-scatter.10.cloned.1.call-done = f32[32,512]{1,0:T(8,128)} async-done(((f32[128,512]{1,0:T(8,128)}), f32[32,512]{1,0:T(8,128)}) %reduce-scatter.10.cloned.1.call-update) | async-done | bytes 65552
  257.9 32.4 %reduce-scatter.6.cloned.1.call-done = f32[256,512]{1,0:T(8,128)} async-done(((f32[1024,512]{1,0:T(8,128)}), f32[256,512]{1,0:T(8,128)}) %reduce-scatter.6.cloned.1.call-update) | async-done | bytes 524304 | tf_op jit(solution)/shard_map/reduce_scatter | solution.py:51
  (3 shorter events, 0.1 us)
Async XLA Ops:
  7.2 86.6 %all-gather.3.cloned.1.call-start = ((), (), s32[]{:S(2)}) async-start(), calls=%async_computation.3 | async-start | bytes 5242880 | tf_op jit(solution)/shard_map/all_gather | solution.py:30
  10.2 1.5 copy-start.2
  10.2 187.7 %all-gather.5.cloned.1.call-start = ((), (), s32[]{:S(2)}) async-start(), calls=%async_computation.4 | async-start | bytes 12582912 | tf_op jit(solution)/shard_map/all_gather | solution.py:26
  10.9 224.2 %reduce-scatter.8.cloned.1.call-start = ((), (), s32[]{:S(2)}) async-start(), calls=%async_computation.6 | async-start | bytes 1310720 | tf_op jit(solution)/shard_map/reduce_scatter | solution.py:52
  197.8 10.5 %copy-start = (bf16[1,1024,512]{2,1,0:T(8,128)(2,1)S(1)}, bf16[1,1024,512]{2,1,0:T(8,128)(2,1)}, u32[]{:S(2)}) copy-start(bf16[1,1024,512]{2,1,0:T(8,128)(2,1)} %get-tuple-element.6) | copy-start | bytes 3145732
  209.2 1.0 copy-start.1
  210.2 47.7 %reduce-scatter.10.cloned.1.call-start = ((), (), s32[]{:S(2)}) async-start(), calls=%async_computation.7 | async-start | bytes 327680
  237.0 53.3 %reduce-scatter.6.cloned.1.call-start = ((), (), s32[]{:S(2)}) async-start(), calls=%async_computation.5 | async-start | bytes 2621440 | tf_op jit(solution)/shard_map/reduce_scatter | solution.py:51
Sparse Core Ops, SparseCore 0:
  10.3 83.4 all-gather.2
  95.3 102.4 all-gather.4
  210.3 24.8 reduce-scatter.7
  237.8 19.9 reduce-scatter.9
  260.8 29.4 reduce-scatter.5
where the time goes:
time: 297 us
  waiting for transfers between devices  265 us (89%)
  between operations  14.5 us (5%)
  matrix products  14.1 us (5%)
    all_gather x1, waiting for transfers between devices, body(): whole_rows = lax.all_gather(green, 'col', axis=2, tiled=True)  104 us
    all_gather x1, waiting for transfers between devices, body(): lax.all_gather(masked, 'row', axis=1, tiled=True)  82 us
    reduce_scatter x1, waiting for transfers between devices, body(): lax.psum_scatter(off_term, 'pole', scatter_dimension=0, tiled=True)  32.4 us
    reduce_scatter x1, waiting for transfers between devices, body(): lax.psum_scatter(diag_term, 'pole', scatter_dimension=0, tiled=True)  24.9 us
    unnamed x6, waiting for transfers between devices  21.6 us
    dot_general x1, matrix products, body(): jnp.einsum('pij,pjk->pik', whole_rows, lax.all_gather(masked, 'row', axis...  10.5 us
  transfers between devices with their start and end apart: 5, of which 5 were waited for; matrix products, arithmetic and copies ran while one was open for 0% of the time, Pallas kernels for 0%

commit v1 on v0

--- a/solution.py
+++ b/solution.py
@@ -24,11 +24,29 @@
     keep_mask = jnp.dot(jnp.dot(row_onehot, pattern_f), col_onehot.T)
     masked = factor * keep_mask.astype(jnp.bfloat16)[None]
     whole_rows = lax.all_gather(green, "col", axis=2, tiled=True)
-    product = jnp.einsum(
-        "pij,pjk->pik",
-        whole_rows,
-        lax.all_gather(masked, "row", axis=1, tiled=True),
-        preferred_element_type=jnp.float32,
+
+    def load_slot_on(x0, mesh_name, dim_i, w_in):
+        now = lax.axis_size(mesh_name)
+        extra, low = (now, lax.axis_index(mesh_name))
+        queue = [(num, (num - 1) % extra) for num in range(extra)]
+        z = x0
+        response = x0.shape[dim_i]
+        block_next = w_in(z, low * response)
+        for dd in range(1, extra):
+            z = lax.ppermute(z, mesh_name, queue)
+            block_next = block_next + w_in(z, (low + dd) % extra * response)
+        return block_next
+
+    product = load_slot_on(
+        masked,
+        "row",
+        1,
+        lambda own_block, at: jnp.einsum(
+            "pij,pjk->pik",
+            lax.dynamic_slice_in_dim(whole_rows, at, own_block.shape[1], axis=2),
+            own_block,
+            preferred_element_type=jnp.float32,
+        ),
     )
     update = (product * keep_mask[None]).astype(jnp.bfloat16)
     weights = pole_weight[:, None, None]

time: 297 us -> 216 us (0.73)
  waiting for transfers between devices: 265 us -> 171 us
  starting transfers between devices: 0.2 us -> 13.8 us
    all_gather x1 -> x0, waiting for transfers between devices: 82 us -> none  [body(): lax.all_gather(masked, 'row', axis=1, tiled=True)]
    all_gather x1, waiting for transfers between devices: 104 us -> 47.4 us  [body(): whole_rows = lax.all_gather(green, 'col', axis=2, tiled=True)]
    ppermute x0 -> x3, waiting for transfers between devices: none -> 44.3 us  [load_slot_on(): z = lax.ppermute(z, mesh_name, queue)]
    ppermute x0 -> x3, starting transfers between devices: none -> 13.6 us  [load_slot_on(): z = lax.ppermute(z, mesh_name, queue)]
    dot_general x1 -> x4, matrix products: 10.5 us -> 9.79 us  [body(): jnp.einsum('pij,pjk->pik', lax.dynamic_slice_in_dim(whole_rows, at, own_b...]
    unnamed x6 -> x5, waiting for transfers between devices: 21.6 us -> 21.7 us
  transfers between devices with their start and end apart: 5 -> 7, of which waited for: 5 -> 6; matrix products, arithmetic and copies ran while one was open for 0% -> 4% of each run, Pallas kernels for 0% -> 0%
where the time goes in v1:
time: 216 us
  waiting for transfers between devices  171 us (79%)
  between operations  14.6 us (7%)
  starting transfers between devices  13.8 us (6%)
  matrix products  12.2 us (6%)
  local copies, waits for them, and re-layouts  4.42 us (2%)
    all_gather x1, waiting for transfers between devices, body(): whole_rows = lax.all_gather(green, 'col', axis=2, tiled=True)  47.4 us
    ppermute x3, waiting for transfers between devices, load_slot_on(): z = lax.ppermute(z, mesh_name, queue)  44.3 us
    reduce_scatter x1, waiting for transfers between devices, body(): lax.psum_scatter(off_term, 'pole', scatter_dimension=0, tiled=True)  32.4 us
    reduce_scatter x1, waiting for transfers between devices, body(): lax.psum_scatter(diag_term, 'pole', scatter_dimension=0, tiled=True)  24.9 us
    unnamed x5, waiting for transfers between devices  21.7 us
    ppermute x3, starting transfers between devices, load_slot_on(): z = lax.ppermute(z, mesh_name, queue)  13.6 us
    dot_general x4, matrix products, body(): jnp.einsum('pij,pjk->pik', lax.dynamic_slice_in_dim(whole_rows, at, own_b...  9.79 us
    unnamed x19, local copies, waits for them, and re-layouts  4.42 us
  transfers between devices with their start and end apart: 7, of which 6 were waited for; matrix products, arithmetic and copies ran while one was open for 4% of the time, Pallas kernels for 0%

profile of v1, /device:TPU:0, one launch (start us, length us, event | category | flops | bytes accessed | tf_op | source)
XLA Modules:
  0.0 215.8 jit_solution(4423911990185290225)
XLA Ops:
  7.2 0.0 copy-start.1
  7.2 0.0 copy-start.5
  7.2 0.0 all-gather.2.cloned.1.call-start
  7.2 0.7 all-gather.2.cloned.1.call-update
  7.9 0.0 reduce-scatter.8.cloned.1.call-start
  8.0 0.4 copy-done.1
  8.4 0.0 copy-done.5
  8.4 0.0 copy-start.4
  8.4 1.7 bitcast_multiply_fusion
  10.1 5.1 %collective-permute-start = (bf16[1,1024,512]{2,1,0:T(8,128)(2,1)}, bf16[1,1024,512]{2,1,0:T(8,128)(2,1)S(1)}, u32[]{:S(2)}, u32[]{:S(2)}) collective-permute-start(bf16[1,1024,512]{2,1,0:T(8,128)(2,1)} %get-tuple-element.6), channel_id=1, source_target_pairs={{0,6},{2,0},{4,2},{6,4},{1,7},{3,1},{5,3},{7,5},{8,14},{10,8},{12,... | collective-permute-start | bytes 3145736 | tf_op jit(solution)/shard_map/ppermute | solution.py:36
  15.2 22.7 %collective-permute-done = bf16[1,1024,512]{2,1,0:T(8,128)(2,1)S(1)} collective-permute-done((bf16[1,1024,512]{2,1,0:T(8,128)(2,1)}, bf16[1,1024,512]{2,1,0:T(8,128)(2,1)S(1)}, u32[]{:S(2)}, u32[]{:S(2)}) %collective-permute-start) | collective-permute-done | bytes 1048608 | tf_op jit(solution)/shard_map/ppermute | solution.py:36
  37.9 0.0 copy-start.6
  37.9 4.2 %collective-permute-start.1 = (bf16[1,1024,512]{2,1,0:T(8,128)(2,1)S(1)}, bf16[1,1024,512]{2,1,0:T(8,128)(2,1)}, u32[]{:S(2)}, u32[]{:S(2)}) collective-permute-start(bf16[1,1024,512]{2,1,0:T(8,128)(2,1)S(1)} %collective-permute-done), channel_id=1, source_target_pairs={{0,6},{2,0},{4,2},{6,4},{1,7},{3,1},{5,3},{7,5},{8,14},{10,8},{12,... | collective-permute-start | bytes 3145736 | tf_op jit(solution)/shard_map/ppermute | solution.py:36
  42.1 21.6 %collective-permute-done.1 = bf16[1,1024,512]{2,1,0:T(8,128)(2,1)} collective-permute-done((bf16[1,1024,512]{2,1,0:T(8,128)(2,1)S(1)}, bf16[1,1024,512]{2,1,0:T(8,128)(2,1)}, u32[]{:S(2)}, u32[]{:S(2)}) %collective-permute-start.1) | collective-permute-done | bytes 1048608 | tf_op jit(solution)/shard_map/ppermute | solution.py:36
  63.6 4.4 %collective-permute-start.2 = (bf16[1,1024,512]{2,1,0:T(8,128)(2,1)}, bf16[1,1024,512]{2,1,0:T(8,128)(2,1)}, u32[]{:S(2)}, u32[]{:S(2)}) collective-permute-start(bf16[1,1024,512]{2,1,0:T(8,128)(2,1)} %collective-permute-done.1), channel_id=1, source_target_pairs={{0,6},{2,0},{4,2},{6,4},{1,7},{3,1},{5,3},{7,5},{8,14},{10,8},{12,... | collective-permute-start | bytes 3145736 | tf_op jit(solution)/shard_map/ppermute | solution.py:36
  68.0 0.0 copy-done.6
  68.7 0.0 copy-done.4
  68.7 0.1 copy.9
  68.8 0.0 copy-start.2
  68.8 47.4 %all-gather.2.cloned.1.call-done = bf16[1,1024,4096]{2,1,0:T(8,128)(2,1)} async-done(((bf16[1,1024,2048]{2,1,0:T(8,128)(2,1)}), bf16[1,1024,4096]{2,1,0:T(8,128)(2,1)}) %all-gather.2.cloned.1.call-update) | async-done | bytes 8388624 | tf_op jit(solution)/shard_map/all_gather | solution.py:26
  116.3 0.0 copy-start.3
  116.3 3.3 %fusion.2 = f32[1024,512]{1,0:T(8,128)S(1)} fusion(bf16[1,1024,4096]{2,1,0:T(8,128)(2,1)} %all-gather.2.cloned.1.call-done, s32[]{:T(128)S(6)} %select_n.55, bf16[1,1024,512]{2,1,0:T(8,128)(2,1)} %collective-permute-done.1), kind=kOutput, calls=%fused_computation.2 | convolution fusion | flops 1073741824 | bytes 5242884 | tf_op jit(solution)/shard_map/pij,pjk->pik/dot_general | solution.py:44
  119.5 0.0 copy-done.2
  119.5 1.1 copy-done.3
  120.6 0.0 copy-start.7
  120.6 1.2 fusion.6
  121.9 0.0 copy-done.7
  121.9 1.3 fusion.4
  123.1 0.0 collective-permute-done.2
  123.1 4.0 %multiply_negate_fusion = (f32[1024,512]{1,0:T(8,128)}, bf16[1024,512]{1,0:T(8,128)(2,1)S(1)}) fusion(f32[]{:T(128)} %bitcast.52, f32[1024,512]{1,0:T(8,128)S(1)} %get-tuple-element.7, bf16[1,1024,512]{2,1,0:T(8,128)(2,1)} %collective-permute-done.2, bf16[1,1024,4096]{2,1,0:T(8,128)(2,1)S(1)} %copy-done.3, s32[]{:T(128)S(6)} %select_n.57, ...), kind=kOutput, calls=%fused_computation.8 | convolution fusion | flops 1077936128 | bytes 14680072 | tf_op jit(solution)/shard_map/pij,pjk->pik/dot_general | solution.py:44
  127.2 0.7 fusion.14
  127.9 0.1 copy.13
  128.1 0.0 copy-start
  128.1 1.0 copy-done
  129.0 0.0 reduce-scatter.8.cloned.1.call-update
  129.0 0.0 reduce-scatter.10.cloned.1.call-start
  129.1 24.9 %reduce-scatter.8.cloned.1.call-done = f32[128,512]{0,1:T(8,128)} async-done(((f32[512,512]{0,1:T(8,128)}), f32[128,512]{0,1:T(8,128)}) %reduce-scatter.8.cloned.1.call-update) | async-done | bytes 262160 | tf_op jit(solution)/shard_map/reduce_scatter | solution.py:70
  154.0 1.8 copy.11
  155.8 0.0 reduce-scatter.10.cloned.1.call-update
  155.8 0.0 reduce-scatter.6.cloned.1.call-start
  155.9 0.5 reduce-scatter.6.cloned.1.call-update
  156.4 20.5 %reduce-scatter.10.cloned.1.call-done = f32[32,512]{1,0:T(8,128)} async-done(((f32[128,512]{1,0:T(8,128)}), f32[32,512]{1,0:T(8,128)}) %reduce-scatter.10.cloned.1.call-update) | async-done | bytes 65552
  176.8 32.4 %reduce-scatter.6.cloned.1.call-done = f32[256,512]{1,0:T(8,128)} async-done(((f32[1024,512]{1,0:T(8,128)}), f32[256,512]{1,0:T(8,128)}) %reduce-scatter.6.cloned.1.call-update) | async-done | bytes 524304 | tf_op jit(solution)/shard_map/reduce_scatter | solution.py:69
  (3 shorter events, 0.1 us)
Async XLA Ops:
  7.2 1.2 copy-start.1
  7.2 1.2 copy-start.5
  7.2 109.1 %all-gather.2.cloned.1.call-start = ((), (), s32[]{:S(2)}) async-start(), calls=%async_computation.3 | async-start | bytes 12582912 | tf_op jit(solution)/shard_map/all_gather | solution.py:26
  7.9 146.1 %reduce-scatter.8.cloned.1.call-start = ((), (), s32[]{:S(2)}) async-start(), calls=%async_computation.5 | async-start | bytes 1310720 | tf_op jit(solution)/shard_map/reduce_scatter | solution.py:70
  8.4 60.3 %copy-start.4 = (bf16[1,128,512]{2,1,0:T(8,128)(2,1)S(1)}, bf16[1,128,512]{2,1,0:T(8,128)(2,1)}, u32[]{:S(2)}) copy-start(bf16[1,128,512]{2,1,0:T(8,128)(2,1)} %param.7) | copy-start | bytes 393220
  10.1 27.8 %collective-permute-start = (bf16[1,1024,512]{2,1,0:T(8,128)(2,1)}, bf16[1,1024,512]{2,1,0:T(8,128)(2,1)S(1)}, u32[]{:S(2)}, u32[]{:S(2)}) collective-permute-start(bf16[1,1024,512]{2,1,0:T(8,128)(2,1)} %get-tuple-element.6), channel_id=1, source_target_pairs={{0,6},{2,0},{4,2},{6,4},{1,7},{3,1},{5,3},{7,5},{8,14},{10,8},{12,... | collective-permute-start | bytes 3145736 | tf_op jit(solution)/shard_map/ppermute | solution.py:36
  37.9 30.1 %copy-start.6 = (bf16[1,1024,512]{2,1,0:T(8,128)(2,1)}, bf16[1,1024,512]{2,1,0:T(8,128)(2,1)S(1)}, u32[]{:S(2)}) copy-start(bf16[1,1024,512]{2,1,0:T(8,128)(2,1)S(1)} %collective-permute-done) | copy-start | bytes 3145732
  37.9 25.7 %collective-permute-start.1 = (bf16[1,1024,512]{2,1,0:T(8,128)(2,1)S(1)}, bf16[1,1024,512]{2,1,0:T(8,128)(2,1)}, u32[]{:S(2)}, u32[]{:S(2)}) collective-permute-start(bf16[1,1024,512]{2,1,0:T(8,128)(2,1)S(1)} %collective-permute-done), channel_id=1, source_target_pairs={{0,6},{2,0},{4,2},{6,4},{1,7},{3,1},{5,3},{7,5},{8,14},{10,8},{12,... | collective-permute-start | bytes 3145736 | tf_op jit(solution)/shard_map/ppermute | solution.py:36
  63.6 59.5 %collective-permute-start.2 = (bf16[1,1024,512]{2,1,0:T(8,128)(2,1)}, bf16[1,1024,512]{2,1,0:T(8,128)(2,1)}, u32[]{:S(2)}, u32[]{:S(2)}) collective-permute-start(bf16[1,1024,512]{2,1,0:T(8,128)(2,1)} %collective-permute-done.1), channel_id=1, source_target_pairs={{0,6},{2,0},{4,2},{6,4},{1,7},{3,1},{5,3},{7,5},{8,14},{10,8},{12,... | collective-permute-start | bytes 3145736 | tf_op jit(solution)/shard_map/ppermute | solution.py:36
  68.8 50.7 %copy-start.2 = (bf16[1,1024,512]{2,1,0:T(8,128)(2,1)S(1)}, bf16[1,1024,512]{2,1,0:T(8,128)(2,1)}, u32[]{:S(2)}) copy-start(bf16[1,1024,512]{2,1,0:T(8,128)(2,1)} %get-tuple-element.6) | copy-start | bytes 3145732
  116.3 4.3 %copy-start.3 = (bf16[1,1024,4096]{2,1,0:T(8,128)(2,1)S(1)}, bf16[1,1024,4096]{2,1,0:T(8,128)(2,1)}, u32[]{:S(2)}) copy-start(bf16[1,1024,4096]{2,1,0:T(8,128)(2,1)} %all-gather.2.cloned.1.call-done) | copy-start | bytes 25165828
  120.6 1.2 copy-start.7
  128.1 1.0 copy-start
  129.0 47.8 %reduce-scatter.10.cloned.1.call-start = ((), (), s32[]{:S(2)}) async-start(), calls=%async_computation.6 | async-start | bytes 327680
  155.8 53.4 %reduce-scatter.6.cloned.1.call-start = ((), (), s32[]{:S(2)}) async-start(), calls=%async_computation.4 | async-start | bytes 2621440 | tf_op jit(solution)/shard_map/reduce_scatter | solution.py:69
Sparse Core Ops, SparseCore 0:
  9.5 106.6 all-gather.1
  129.2 24.7 reduce-scatter.7
  156.8 19.9 reduce-scatter.9
  179.8 29.4 reduce-scatter.5
